TPU v7x, 512 devices: a whole 4x8x8 slice. The times are simulated.
512 devices in a mesh: layer: 32 (over x_lo, y, core), tp: 16 (over z, x_hi).
Axes of the slice: x: 4 (x_hi: 2, x_lo: 2; x = x_hi * 2 + x_lo), y: 8, z: 8, core: 2. Of those that a mesh axis runs over, the one named last changes fastest.
Arguments:
- acts: bfloat16 [4096, 2048], P(('layer', 'tp')), may hold values from -12 to 12, as said below
- fresh: bfloat16 [2, 128, 2048], P(None, 'tp'), may hold values from -12 to 12, as said below
- norm_first: float32 [16, 2048], replicated, may hold values from 0.5 to 1.5
- norm_second: float32 [16, 2048], replicated, may hold values from 0.5 to 1.5
- proj_qkv: bfloat16 [512, 2048, 192], P(('layer', 'tp')), may hold values from -1 to 1
- proj_out: bfloat16 [32768, 2048], P(('layer', 'tp')), may hold values from -0.125 to 0.125
- proj_gate_up: bfloat16 [2048, 2, 131072], P(None, None, ('layer', 'tp')), may hold values from -0.125 to 0.125
- proj_down: bfloat16 [131072, 2048], P(('layer', 'tp')), may hold values from -0.0625 to 0.0625
- memory_state: float32 [512, 64, 64], P(('layer', 'tp')), may hold values from -768 to 768
- memory_norm: float32 [512, 64], P(('layer', 'tp')), may hold values from 16 to 256
- bias_gate: float32 [512], P(('layer', 'tp')), may hold values from -3 to 3
Outputs:
- first_out: bfloat16 [4096, 2048], P(('layer', 'tp'))
- second_out: bfloat16 [4096, 2048], P(('layer', 'tp'))
- memory_after: float32 [512, 64, 64], P(('layer', 'tp'))
- norm_after: float32 [512, 64], P(('layer', 'tp'))
Inputs may be any that keep to these rules, and one draw needn't show every extreme that they name: `acts`: activation rows. `fresh`: activation rows.
All inputs are finite; a program needn't handle non-finite values.
Results may differ from a plain program's by a relative error of at most 0.025.
Values may be sent and summed in bfloat16 or wider, within the bound.
No kernel may reach another device: no remote copies, remote signals or barrier semaphores. Data moves between devices by JAX's collectives and lax.ppermute only.
A program may use at most 64 MiB of HBM per device.

v0:
```python
import jax
import jax.numpy as jnp
from jax import lax
from jax.sharding import PartitionSpec as P


def partner_2(value, axis, distance):
    mask = 2**distance
    pairs = [(source, source ^ mask) for source in range(lax.axis_size(axis))]
    return lax.ppermute(value, axis, pairs)


def shifted(value, axis, steps):
    count = lax.axis_size(axis)
    initial, last = (max(0, -steps), min(count, count - steps))
    return lax.ppermute(value, axis, [(source, source + steps) for source in range(initial, last)])


def rms_norm(values, weight):
    floats = values.astype(jnp.float32)
    scaled = floats * lax.rsqrt(jnp.mean(floats * floats, axis=-1, keepdims=True) + 1e-05)
    return (scaled * weight).astype(jnp.bfloat16)


def attend(qkv, memory, totals, logits):
    head_dim = memory.shape[-1]
    seg_len = qkv.shape[0]
    queries = qkv[..., :head_dim]
    keyed = qkv[..., head_dim : 2 * head_dim]
    valued = qkv[..., 2 * head_dim :]
    scores = jnp.einsum(
        "qhc,khc->hqk", queries, keyed, preferred_element_type=jnp.float32
    ) * head_dim ** (-0.5)
    positions = jnp.arange(seg_len)
    allowed = positions[:, None] >= positions[None, :]
    probs = jax.nn.softmax(jnp.where(allowed[None], scores, -jnp.inf), axis=-1).astype(jnp.bfloat16)
    direct = jnp.einsum("hqk,khc->qhc", probs, valued, preferred_element_type=jnp.float32)
    lifted_q = jax.nn.elu(queries.astype(jnp.float32)) + 1.0
    lifted_k = jax.nn.elu(keyed.astype(jnp.float32)) + 1.0
    numer = jnp.einsum("qhc,hce->qhe", lifted_q, memory, precision=lax.Precision.HIGHEST)
    denom = jnp.einsum("qhc,hc->qh", lifted_q, totals, precision=lax.Precision.HIGHEST)[..., None]
    gate_open = jax.nn.sigmoid(logits)[None, :, None]
    blended = (gate_open * numer / denom + (1.0 - gate_open) * direct).astype(jnp.bfloat16)
    new_memory = memory + jnp.einsum(
        "khc,khe->hce", lifted_k, valued.astype(jnp.float32), precision=lax.Precision.HIGHEST
    )
    new_totals = totals + jnp.sum(lifted_k, axis=0)
    return (blended.reshape(seg_len, -1), new_memory, new_totals)


def body(
    acts,
    fresh,
    norm_first,
    norm_second,
    proj_qkv,
    proj_out,
    proj_gate_up,
    proj_down,
    memory_state,
    memory_norm,
    bias_gate,
):
    position = lax.axis_index("layer")
    lower = position % 2 == 0
    depth = position // 2
    member = lax.axis_index("tp")
    gain_one = lax.dynamic_index_in_dim(norm_first, depth, 0, keepdims=False)
    gain_two = lax.dynamic_index_in_dim(norm_second, depth, 0, keepdims=False)
    row_count = acts.shape[0]

    def ordered(mine, other):
        return jnp.concatenate(
            [jnp.where(lower, mine, other), jnp.where(lower, other, mine)], axis=0
        )

    def project(rows):
        return jnp.einsum("sd,hdc->shc", rows, proj_qkv, preferred_element_type=jnp.float32).astype(
            jnp.bfloat16
        )

    def expand(rows):
        gate_up = jnp.einsum("sd,dtf->stf", rows, proj_gate_up, preferred_element_type=jnp.float32)
        return (jax.nn.silu(gate_up[:, 0]) * gate_up[:, 1]).astype(jnp.bfloat16)

    def collect_all(values):
        partner = partner_2(values, "layer", 0)
        mine, other = (
            lax.all_gather(values, "tp", axis=0, tiled=True),
            lax.all_gather(partner, "tp", axis=0, tiled=True),
        )
        return ordered(mine, other)

    def total_all(local, weight):
        summed = lax.psum(
            jnp.dot(local, weight, preferred_element_type=jnp.float32).astype(jnp.bfloat16), "tp"
        ).astype(jnp.float32)
        return summed + partner_2(summed.astype(jnp.bfloat16), "layer", 0).astype(summed.dtype)

    def apply_layer(stream, memory, totals):
        gathered = collect_all(stream)
        seg_len = gathered.shape[0]
        qkv = project(rms_norm(gathered, gain_one))
        blended, memory, totals = attend(qkv, memory, totals, bias_gate)
        attn = total_all(blended, proj_out)
        hidden_one = (gathered.astype(jnp.float32) + attn).astype(jnp.bfloat16)
        hidden = expand(rms_norm(hidden_one, gain_two))
        ffn = total_all(hidden, proj_down)
        complete = (hidden_one.astype(jnp.float32) + ffn).astype(jnp.bfloat16)
        start = position % 2 * (seg_len // 2) + member * row_count
        output = lax.dynamic_slice_in_dim(complete, start, row_count, 0)
        return (output, memory, totals)

    first_rows, memory_one, totals_one = apply_layer(acts, memory_state, memory_norm)
    incoming = shifted(first_rows, "layer", 2)
    fresh_rows = lax.dynamic_index_in_dim(fresh, position % 2, 0, keepdims=False)
    entering = jnp.where(depth == 0, fresh_rows, incoming)
    second_rows, memory_two, totals_two = apply_layer(entering, memory_one, totals_one)
    return (first_rows, second_rows, memory_two, totals_two)


def solution(mesh):
    in_specs = (
        P(("layer", "tp"), None),
        P(None, "tp", None),
        P(),
        P(),
        P(("layer", "tp"), None, None),
        P(("layer", "tp"), None),
        P(None, None, ("layer", "tp")),
        P(("layer", "tp"), None),
        P(("layer", "tp"), None, None),
        P(("layer", "tp"), None),
        P(("layer", "tp")),
    )
    out_specs = (
        P(("layer", "tp"), None),
        P(("layer", "tp"), None),
        P(("layer", "tp"), None, None),
        P(("layer", "tp"), None),
    )
    return jax.shard_map(body, mesh=mesh, in_specs=in_specs, out_specs=out_specs, check_vma=False)
```

profile of v0, /device:TPU:1, one launch (start us, length us, event | category | flops | bytes accessed | tf_op | source)
XLA Modules:
  0.0 903.9 jit_solution(7788227879883312457)
XLA Ops:
  7.2 8.9 collective-permute-start
  16.1 40.0 %all_gather.12 = bf16[128,2048]{1,0:T(8,128)(2,1)} all-gather(bf16[8,2048]{1,0:T(8,128)(2,1)} %param.11), channel_id=1, replica_groups=mesh['layer'=32,'tp'=16] {'tp'}, dimensions={0}, use_global_device_ids=true | all-gather | bytes 557056 | tf_op jit(solution)/shard_map/all_gather | solution.py:89
  56.1 0.8 constant_dynamic-slice_fusion.1
  57.7 31.6 %all_gather.13 = bf16[128,2048]{1,0:T(8,128)(2,1)S(1)} all-gather(bf16[8,2048]{1,0:T(8,128)(2,1)S(1)} %collective-permute-done), channel_id=1, replica_groups=mesh['layer'=32,'tp'=16] {'tp'}, dimensions={0}, use_global_device_ids=true | all-gather | bytes 557056 | tf_op jit(solution)/shard_map/all_gather | solution.py:90
  89.3 1.1 broadcast_select_fusion.3
  90.7 1.7 fusion.14
  93.3 2.7 convolution_convert_fusion.3
  96.1 167.5 %all-reduce.5.cloned.1.call-done = bf16[256,2048]{1,0:T(8,128)(2,1)} async-done(((bf16[256,2048]{1,0:T(8,128)(2,1)}), bf16[256,2048]{1,0:T(8,128)(2,1)}) %all-reduce.5.cloned.1.call-update) | async-done | bytes 1048592 | tf_op jit(solution)/shard_map/psum | solution.py:95
  263.6 13.1 %collective-permute-start.1 = (bf16[256,2048]{1,0:T(8,128)(2,1)}, bf16[256,2048]{1,0:T(8,128)(2,1)S(1)}, u32[]{:S(2)}, u32[]{:S(2)}) collective-permute-start(bf16[256,2048]{1,0:T(8,128)(2,1)} %all-reduce.5.cloned.1.call-done), channel_id=1, source_target_pairs={{0,16},{16,0},{32,48},{48,32},{64,80},{80,64},{96,112},{112,96},{1... | collective-permute-start | bytes 3145736 | tf_op jit(solution)/shard_map/ppermute | solution.py:10
  276.7 0.9 constant_dynamic-slice_fusion
  277.5 1.6 collective-permute-done.1
  279.2 1.8 multiply_reduce_fusion.1
  283.0 1.5 convolution_convert_fusion.1
  284.5 153.8 %all-reduce.7.cloned.1.call-done = bf16[256,2048]{1,0:T(8,128)(2,1)} async-done(((bf16[256,2048]{1,0:T(8,128)(2,1)}), bf16[256,2048]{1,0:T(8,128)(2,1)}) %all-reduce.7.cloned.1.call-update) | async-done | bytes 1048592 | tf_op jit(solution)/shard_map/psum | solution.py:95
  438.3 13.1 %collective-permute-start.2 = (bf16[256,2048]{1,0:T(8,128)(2,1)}, bf16[256,2048]{1,0:T(8,128)(2,1)S(1)}, u32[]{:S(2)}, u32[]{:S(2)}) collective-permute-start(bf16[256,2048]{1,0:T(8,128)(2,1)} %all-reduce.7.cloned.1.call-done), channel_id=1, source_target_pairs={{0,16},{16,0},{32,48},{48,32},{64,80},{80,64},{96,112},{112,96},{1... | collective-permute-start | bytes 3145736 | tf_op jit(solution)/shard_map/ppermute | solution.py:10
  451.7 2.2 collective-permute-done.2
  453.9 0.9 fusion.77
  454.8 3.1 collective-permute-start.3
  458.0 0.9 collective-permute-done.3
  458.9 3.3 collective-permute-start.4
  462.2 36.4 %all_gather.14 = bf16[128,2048]{1,0:T(8,128)(2,1)S(1)} all-gather(bf16[8,2048]{1,0:T(8,128)(2,1)S(1)} %bitcast_select_fusion), channel_id=1, replica_groups=mesh['layer'=32,'tp'=16] {'tp'}, dimensions={0}, use_global_device_ids=true | all-gather | bytes 557056 | tf_op jit(solution)/shard_map/all_gather | solution.py:89
  498.7 32.0 %all_gather.15 = bf16[128,2048]{1,0:T(8,128)(2,1)S(1)} all-gather(bf16[8,2048]{1,0:T(8,128)(2,1)S(1)} %collective-permute-done.4), channel_id=1, replica_groups=mesh['layer'=32,'tp'=16] {'tp'}, dimensions={0}, use_global_device_ids=true | all-gather | bytes 557056 | tf_op jit(solution)/shard_map/all_gather | solution.py:90
  532.6 2.6 convolution_convert_fusion.2
  535.3 170.2 %all-reduce.9.cloned.1.call-done = bf16[256,2048]{1,0:T(8,128)(2,1)} async-done(((bf16[256,2048]{1,0:T(8,128)(2,1)}), bf16[256,2048]{1,0:T(8,128)(2,1)}) %all-reduce.9.cloned.1.call-update) | async-done | bytes 1048592 | tf_op jit(solution)/shard_map/psum | solution.py:95
  705.5 13.1 %collective-permute-start.5 = (bf16[256,2048]{1,0:T(8,128)(2,1)}, bf16[256,2048]{1,0:T(8,128)(2,1)S(1)}, u32[]{:S(2)}, u32[]{:S(2)}) collective-permute-start(bf16[256,2048]{1,0:T(8,128)(2,1)} %all-reduce.9.cloned.1.call-done), channel_id=1, source_target_pairs={{0,16},{16,0},{32,48},{48,32},{64,80},{80,64},{96,112},{112,96},{1... | collective-permute-start | bytes 3145736 | tf_op jit(solution)/shard_map/ppermute | solution.py:10
  718.6 2.5 collective-permute-done.5
  721.0 1.8 multiply_reduce_fusion
  724.8 1.4 convolution_convert_fusion
  726.3 154.0 %all-reduce.11.cloned.1.call-done = bf16[256,2048]{1,0:T(8,128)(2,1)} async-done(((bf16[256,2048]{1,0:T(8,128)(2,1)}), bf16[256,2048]{1,0:T(8,128)(2,1)}) %all-reduce.11.cloned.1.call-update) | async-done | bytes 1048592 | tf_op jit(solution)/shard_map/psum | solution.py:95
  880.3 13.1 %collective-permute-start.6 = (bf16[256,2048]{1,0:T(8,128)(2,1)}, bf16[256,2048]{1,0:T(8,128)(2,1)S(1)}, u32[]{:S(2)}, u32[]{:S(2)}) collective-permute-start(bf16[256,2048]{1,0:T(8,128)(2,1)} %all-reduce.11.cloned.1.call-done), channel_id=1, source_target_pairs={{0,16},{16,0},{32,48},{48,32},{64,80},{80,64},{96,112},{112,96},{1... | collective-permute-start | bytes 3145736 | tf_op jit(solution)/shard_map/ppermute | solution.py:10
  894.8 1.0 collective-permute-done.6
  895.9 1.5 fusion.76
  (68 shorter events, 9.1 us)
Async XLA Ops:
  7.2 273.8 %copy-start = (bf16[2048,2,256]{2,1,0:T(2,128)(2,1)S(1)}, bf16[2048,2,256]{2,1,0:T(2,128)(2,1)}, u32[]{:S(2)}) copy-start(bf16[2048,2,256]{2,1,0:T(2,128)(2,1)} %param.17) | copy-start | bytes 6291460
  7.2 256.4 %all-reduce.5.cloned.1.call-start = ((), (), s32[]{:S(2)}) async-start(), calls=%async_computation | async-start | bytes 2097152 | tf_op jit(solution)/shard_map/psum | solution.py:95
  7.2 50.5 %collective-permute-start = (bf16[8,2048]{1,0:T(8,128)(2,1)}, bf16[8,2048]{1,0:T(8,128)(2,1)S(1)}, u32[]{:S(2)}, u32[]{:S(2)}) collective-permute-start(bf16[8,2048]{1,0:T(8,128)(2,1)} %param.11), channel_id=1, source_target_pairs={{0,16},{16,0},{32,48},{48,32},{64,80},{80,64},{96,112},{112,96},{1... | collective-permute-start | bytes 98312 | tf_op jit(solution)/shard_map/ppermute | solution.py:10
  90.7 2.0 copy-start.9
  90.7 2.4 copy-start.13
  92.4 0.6 copy-start.3
  96.0 342.3 %all-reduce.7.cloned.1.call-start = ((), (), s32[]{:S(2)}) async-start(), calls=%async_computation.1 | async-start | bytes 2097152 | tf_op jit(solution)/shard_map/psum | solution.py:95
  263.6 15.6 %collective-permute-start.1 = (bf16[256,2048]{1,0:T(8,128)(2,1)}, bf16[256,2048]{1,0:T(8,128)(2,1)S(1)}, u32[]{:S(2)}, u32[]{:S(2)}) collective-permute-start(bf16[256,2048]{1,0:T(8,128)(2,1)} %all-reduce.5.cloned.1.call-done), channel_id=1, source_target_pairs={{0,16},{16,0},{32,48},{48,32},{64,80},{80,64},{96,112},{112,96},{1... | collective-permute-start | bytes 3145736 | tf_op jit(solution)/shard_map/ppermute | solution.py:10
  280.9 1.3 copy-start.1
  281.0 2.0 copy-start.10
  282.9 168.5 %copy-start.4 = (bf16[256,1,192]{0,2,1:T(8,128)(2,1)S(1)}, bf16[256,1,192]{0,2,1:T(8,128)(2,1)}, u32[]{:S(2)}) copy-start(bf16[256,1,192]{0,2,1:T(8,128)(2,1)} %copy-done.3) | copy-start | bytes 294916
  282.9 168.5 %copy-start.14 = (f32[1,64,64]{2,1,0:T(8,128)S(1)}, f32[1,64,64]{2,1,0:T(8,128)}, u32[]{:S(2)}) copy-start(f32[1,64,64]{2,1,0:T(8,128)} %param.19) | copy-start | bytes 49156
  283.0 176.0 %copy-start.8 = (bf16[2,8,2048]{2,1,0:T(8,128)(2,1)S(1)}, bf16[2,8,2048]{2,1,0:T(8,128)(2,1)}, u32[]{:S(2)}) copy-start(bf16[2,8,2048]{2,1,0:T(8,128)(2,1)} %param.12) | copy-start | bytes 196612
  284.4 421.0 %all-reduce.9.cloned.1.call-start = ((), (), s32[]{:S(2)}) async-start(), calls=%async_computation.2 | async-start | bytes 2097152 | tf_op jit(solution)/shard_map/psum | solution.py:95
  438.3 15.6 %collective-permute-start.2 = (bf16[256,2048]{1,0:T(8,128)(2,1)}, bf16[256,2048]{1,0:T(8,128)(2,1)S(1)}, u32[]{:S(2)}, u32[]{:S(2)}) collective-permute-start(bf16[256,2048]{1,0:T(8,128)(2,1)} %all-reduce.7.cloned.1.call-done), channel_id=1, source_target_pairs={{0,16},{16,0},{32,48},{48,32},{64,80},{80,64},{96,112},{112,96},{1... | collective-permute-start | bytes 3145736 | tf_op jit(solution)/shard_map/ppermute | solution.py:10
  451.7 80.4 %copy-start.15 = (f32[1,64,64]{2,1,0:T(8,128)}, f32[1,64,64]{2,1,0:T(8,128)S(1)}, u32[]{:S(2)}) copy-start(f32[1,64,64]{2,1,0:T(8,128)S(1)} %fusion.26) | copy-start | bytes 49156
  454.8 76.2 %copy-start.7 = (bf16[8,2048]{1,0:T(8,128)(2,1)}, bf16[8,2048]{1,0:T(8,128)(2,1)S(1)}, u32[]{:S(2)}) copy-start(bf16[8,2048]{1,0:T(8,128)(2,1)S(1)} %fusion.77) | copy-start | bytes 98308
  454.8 4.1 collective-permute-start.3
  458.9 72.1 %copy-start.12 = (bf16[1,2048,192]{1,2,0:T(8,128)(2,1)S(1)}, bf16[1,2048,192]{1,2,0:T(8,128)(2,1)}, u32[]{:S(2)}) copy-start(bf16[1,2048,192]{1,2,0:T(8,128)(2,1)} %param.15) | copy-start | bytes 2359300
  458.9 39.7 %collective-permute-start.4 = (bf16[8,2048]{1,0:T(8,128)(2,1)S(1)}, bf16[8,2048]{1,0:T(8,128)(2,1)S(1)}, u32[]{:S(2)}, u32[]{:S(2)}) collective-permute-start(bf16[8,2048]{1,0:T(8,128)(2,1)S(1)} %bitcast_select_fusion), channel_id=1, source_target_pairs={{0,16},{16,0},{32,48},{48,32},{64,80},{80,64},{96,112},{112,96},{1... | collective-permute-start | bytes 98312 | tf_op jit(solution)/shard_map/ppermute | solution.py:10
  531.6 0.6 copy-start.5
  535.3 345.0 %all-reduce.11.cloned.1.call-start = ((), (), s32[]{:S(2)}) async-start(), calls=%async_computation.3 | async-start | bytes 2097152 | tf_op jit(solution)/shard_map/psum | solution.py:95
  705.5 15.6 %collective-permute-start.5 = (bf16[256,2048]{1,0:T(8,128)(2,1)}, bf16[256,2048]{1,0:T(8,128)(2,1)S(1)}, u32[]{:S(2)}, u32[]{:S(2)}) collective-permute-start(bf16[256,2048]{1,0:T(8,128)(2,1)} %all-reduce.9.cloned.1.call-done), channel_id=1, source_target_pairs={{0,16},{16,0},{32,48},{48,32},{64,80},{80,64},{96,112},{112,96},{1... | collective-permute-start | bytes 3145736 | tf_op jit(solution)/shard_map/ppermute | solution.py:10
  722.8 1.3 copy-start.2
  722.8 2.0 copy-start.11
  724.8 168.5 %copy-start.6 = (bf16[256,1,192]{0,2,1:T(8,128)(2,1)S(1)}, bf16[256,1,192]{0,2,1:T(8,128)(2,1)}, u32[]{:S(2)}) copy-start(bf16[256,1,192]{0,2,1:T(8,128)(2,1)} %copy-done.5) | copy-start | bytes 294916
  724.8 169.2 %copy-start.16 = (f32[1,64,64]{2,1,0:T(8,128)S(1)}, f32[1,64,64]{2,1,0:T(8,128)}, u32[]{:S(2)}) copy-start(f32[1,64,64]{2,1,0:T(8,128)} %copy-done.15) | copy-start | bytes 49156
  880.3 15.6 %collective-permute-start.6 = (bf16[256,2048]{1,0:T(8,128)(2,1)}, bf16[256,2048]{1,0:T(8,128)(2,1)S(1)}, u32[]{:S(2)}, u32[]{:S(2)}) collective-permute-start(bf16[256,2048]{1,0:T(8,128)(2,1)} %all-reduce.11.cloned.1.call-done), channel_id=1, source_target_pairs={{0,16},{16,0},{32,48},{48,32},{64,80},{80,64},{96,112},{112,96},{1... | collective-permute-start | bytes 3145736 | tf_op jit(solution)/shard_map/ppermute | solution.py:10
Sparse Core Ops, SparseCore 0:
  96.1 167.3 all-reduce.4
  284.6 153.7 all-reduce.6
  535.4 170.0 all-reduce.8
  726.4 153.7 all-reduce.10
where the time goes:
time: 905 us; the launch traced here: 904 us
  waiting for transfers between devices  654 us (72%)
  blocking collectives  140 us (15%)
  starting transfers between devices  67.8 us (7%)
  between operations  14.8 us (2%)
  matrix products  14.4 us (2%)
    psum x4, waiting for transfers between devices, total_all(): lax.psum(jnp.dot(local, weight, preferred_element_type=jnp.float32).astyp...  645 us
    all_gather x2, blocking collectives, collect_all(): lax.all_gather(values, 'tp', axis=0, tiled=True)  76.4 us
    ppermute x6, starting transfers between devices, partner_2(): return lax.ppermute(value, axis, pairs)  64.6 us
    all_gather x2, blocking collectives, collect_all(): lax.all_gather(partner, 'tp', axis=0, tiled=True)  63.5 us
  transfers between devices with their start and end apart: 11, of which 9 were waited for; matrix products, arithmetic and copies ran while one was open for 0% of the time, Pallas kernels for 0%

commit v1 on v0

--- a/solution.py
+++ b/solution.py
@@ -2,6 +2,13 @@
 import jax.numpy as jnp
 from jax import lax
 from jax.sharding import PartitionSpec as P
+
+
+def all_by_exchange(x, axis, dim):
+    peers = lax.axis_size(axis)
+    tiles = jnp.stack([x for _ in range(peers)])
+    tiles = lax.all_to_all(tiles, axis, split_axis=0, concat_axis=0)
+    return jnp.concatenate(tiles, axis=dim)
 
 
 def partner_2(value, axis, distance):
@@ -86,7 +93,7 @@
     def collect_all(values):
         partner = partner_2(values, "layer", 0)
         mine, other = (
-            lax.all_gather(values, "tp", axis=0, tiled=True),
+            all_by_exchange(values, "tp", 0),
             lax.all_gather(partner, "tp", axis=0, tiled=True),
         )
         return ordered(mine, other)

time: 905 us -> 854 us (0.944)
  blocking collectives: 140 us -> 83 us
  waiting for transfers between devices: 654 us -> 640 us
  starting transfers between devices: 67.8 us -> 81.4 us
    all_gather x2 -> x0, blocking collectives: 76.4 us -> none  [collect_all(): lax.all_gather(values, 'tp', axis=0, tiled=True)]
    all_gather x2, blocking collectives: 63.5 us -> 83 us  [collect_all(): lax.all_gather(partner, 'tp', axis=0, tiled=True)]
    all_to_all x0 -> x2, starting transfers between devices: none -> 19.4 us  [all_by_exchange(): tiles = lax.all_to_all(tiles, axis, split_axis=0, concat_axis=0)]
    psum x4, waiting for transfers between devices: 645 us -> 631 us  [total_all(): lax.psum(jnp.dot(local, weight, preferred_element_type=jnp.float32).astyp...]
  transfers between devices with their start and end apart: 11 -> 13, of which waited for: 9 -> 10; matrix products, arithmetic and copies ran while one was open for 0% -> 0% of each run, Pallas kernels for 0% -> 0%
where the time goes in v1:
time: 854 us; the launch traced here: 853 us
  waiting for transfers between devices  640 us (75%)
  blocking collectives  83 us (10%)
  starting transfers between devices  81.4 us (10%)
  matrix products  16.1 us (2%)
  between operations  14.8 us (2%)
  other arithmetic  9.98 us (1%)
    psum x4, waiting for transfers between devices, total_all(): lax.psum(jnp.dot(local, weight, preferred_element_type=jnp.float32).astyp...  631 us
    all_gather x2, blocking collectives, collect_all(): lax.all_gather(partner, 'tp', axis=0, tiled=True)  83 us
    ppermute x6, starting transfers between devices, partner_2(): return lax.ppermute(value, axis, pairs)  58.7 us
    all_to_all x2, starting transfers between devices, all_by_exchange(): tiles = lax.all_to_all(tiles, axis, split_axis=0, concat_axis=0)  19.4 us
  transfers between devices with their start and end apart: 13, of which 10 were waited for; matrix products, arithmetic and copies ran while one was open for 0% of the time, Pallas kernels for 0%

profile of v1, /device:TPU:1, one launch (start us, length us, event | category | flops | bytes accessed | tf_op | source)
XLA Modules:
  0.0 852.8 jit_solution(967285610924587074)
XLA Ops:
  7.2 1.8 stack.4
  8.9 13.5 %all-to-all-start = ((bf16[16,8,2048]{2,1,0:T(8,128)(2,1)}), bf16[16,8,2048]{2,1,0:T(8,128)(2,1)}, u32[]{:S(2)}, u32[]{:S(2)}) async-start(bf16[16,8,2048]{2,1,0:T(8,128)(2,1)} %stack.4), calls=%async_computation | async-start | bytes 1048576 | tf_op jit(solution)/shard_map/all_to_all | solution.py:10
  22.5 2.9 collective-permute-start
  27.0 42.1 %all_gather.6 = bf16[128,2048]{1,0:T(8,128)(2,1)} all-gather(bf16[8,2048]{1,0:T(8,128)(2,1)S(1)} %collective-permute-done), channel_id=1, replica_groups=mesh['layer'=32,'tp'=16] {'tp'}, dimensions={0}, use_global_device_ids=true | all-gather | bytes 557056 | tf_op jit(solution)/shard_map/all_gather | solution.py:97
  69.1 1.3 bitcast_select_fusion.3
  70.7 1.7 fusion.14
  73.3 2.6 convolution_convert_fusion.3
  76.0 160.1 %all-reduce.5.cloned.1.call-done = bf16[256,2048]{1,0:T(8,128)(2,1)} async-done(((bf16[256,2048]{1,0:T(8,128)(2,1)}), bf16[256,2048]{1,0:T(8,128)(2,1)}) %all-reduce.5.cloned.1.call-update) | async-done | bytes 1048592 | tf_op jit(solution)/shard_map/psum | solution.py:102
  236.1 13.1 %collective-permute-start.1 = (bf16[256,2048]{1,0:T(8,128)(2,1)}, bf16[256,2048]{1,0:T(8,128)(2,1)S(1)}, u32[]{:S(2)}, u32[]{:S(2)}) collective-permute-start(bf16[256,2048]{1,0:T(8,128)(2,1)} %all-reduce.5.cloned.1.call-done), channel_id=1, source_target_pairs={{0,16},{16,0},{32,48},{48,32},{64,80},{80,64},{96,112},{112,96},{1... | collective-permute-start | bytes 3145736 | tf_op jit(solution)/shard_map/ppermute | solution.py:17
  250.1 1.6 collective-permute-done.1
  251.7 1.8 multiply_reduce_fusion.1
  255.5 1.5 convolution_convert_fusion.1
  257.0 154.3 %all-reduce.7.cloned.1.call-done = bf16[256,2048]{1,0:T(8,128)(2,1)} async-done(((bf16[256,2048]{1,0:T(8,128)(2,1)}), bf16[256,2048]{1,0:T(8,128)(2,1)}) %all-reduce.7.cloned.1.call-update) | async-done | bytes 1048592 | tf_op jit(solution)/shard_map/psum | solution.py:102
  411.2 13.1 %collective-permute-start.2 = (bf16[256,2048]{1,0:T(8,128)(2,1)}, bf16[256,2048]{1,0:T(8,128)(2,1)S(1)}, u32[]{:S(2)}, u32[]{:S(2)}) collective-permute-start(bf16[256,2048]{1,0:T(8,128)(2,1)} %all-reduce.7.cloned.1.call-done), channel_id=1, source_target_pairs={{0,16},{16,0},{32,48},{48,32},{64,80},{80,64},{96,112},{112,96},{1... | collective-permute-start | bytes 3145736 | tf_op jit(solution)/shard_map/ppermute | solution.py:17
  424.4 2.5 collective-permute-done.2
  427.7 3.1 collective-permute-start.3
  430.8 1.0 collective-permute-done.3
  432.7 6.0 all-to-all-start.1
  439.5 3.4 collective-permute-start.4
  443.8 40.8 %all_gather.7 = bf16[128,2048]{1,0:T(8,128)(2,1)} all-gather(bf16[8,2048]{1,0:T(8,128)(2,1)S(1)} %collective-permute-done.4), channel_id=1, replica_groups=mesh['layer'=32,'tp'=16] {'tp'}, dimensions={0}, use_global_device_ids=true | all-gather | bytes 557056 | tf_op jit(solution)/shard_map/all_gather | solution.py:97
  484.6 1.3 bitcast_select_fusion.1
  486.2 1.7 fusion.15
  488.9 2.6 convolution_convert_fusion.2
  491.6 162.4 %all-reduce.9.cloned.1.call-done = bf16[256,2048]{1,0:T(8,128)(2,1)} async-done(((bf16[256,2048]{1,0:T(8,128)(2,1)}), bf16[256,2048]{1,0:T(8,128)(2,1)}) %all-reduce.9.cloned.1.call-update) | async-done | bytes 1048592 | tf_op jit(solution)/shard_map/psum | solution.py:102
  654.0 13.1 %collective-permute-start.5 = (bf16[256,2048]{1,0:T(8,128)(2,1)}, bf16[256,2048]{1,0:T(8,128)(2,1)S(1)}, u32[]{:S(2)}, u32[]{:S(2)}) collective-permute-start(bf16[256,2048]{1,0:T(8,128)(2,1)} %all-reduce.9.cloned.1.call-done), channel_id=1, source_target_pairs={{0,16},{16,0},{32,48},{48,32},{64,80},{80,64},{96,112},{112,96},{1... | collective-permute-start | bytes 3145736 | tf_op jit(solution)/shard_map/ppermute | solution.py:17
  667.2 2.5 collective-permute-done.5
  669.6 1.8 multiply_reduce_fusion
  673.4 1.5 convolution_convert_fusion
  674.9 154.3 %all-reduce.11.cloned.1.call-done = bf16[256,2048]{1,0:T(8,128)(2,1)} async-done(((bf16[256,2048]{1,0:T(8,128)(2,1)}), bf16[256,2048]{1,0:T(8,128)(2,1)}) %all-reduce.11.cloned.1.call-update) | async-done | bytes 1048592 | tf_op jit(solution)/shard_map/psum | solution.py:102
  829.2 13.1 %collective-permute-start.6 = (bf16[256,2048]{1,0:T(8,128)(2,1)}, bf16[256,2048]{1,0:T(8,128)(2,1)S(1)}, u32[]{:S(2)}, u32[]{:S(2)}) collective-permute-start(bf16[256,2048]{1,0:T(8,128)(2,1)} %all-reduce.11.cloned.1.call-done), channel_id=1, source_target_pairs={{0,16},{16,0},{32,48},{48,32},{64,80},{80,64},{96,112},{112,96},{1... | collective-permute-start | bytes 3145736 | tf_op jit(solution)/shard_map/ppermute | solution.py:17
  843.8 1.0 collective-permute-done.6
  844.8 1.5 fusion.76
  (70 shorter events, 13.2 us)
Async XLA Ops:
  7.2 246.3 %copy-start = (bf16[2048,2,256]{2,1,0:T(2,128)(2,1)S(1)}, bf16[2048,2,256]{2,1,0:T(2,128)(2,1)}, u32[]{:S(2)}) copy-start(bf16[2048,2,256]{2,1,0:T(2,128)(2,1)} %param.17) | copy-start | bytes 6291460
  8.9 60.2 %all-to-all-start = ((bf16[16,8,2048]{2,1,0:T(8,128)(2,1)}), bf16[16,8,2048]{2,1,0:T(8,128)(2,1)}, u32[]{:S(2)}, u32[]{:S(2)}) async-start(bf16[16,8,2048]{2,1,0:T(8,128)(2,1)} %stack.4), calls=%async_computation | async-start | bytes 1048576 | tf_op jit(solution)/shard_map/all_to_all | solution.py:10
  22.4 213.7 %all-reduce.5.cloned.1.call-start = ((), (), s32[]{:S(2)}) async-start(), calls=%async_computation.2 | async-start | bytes 2097152 | tf_op jit(solution)/shard_map/psum | solution.py:102
  22.5 4.5 collective-permute-start
  70.7 2.0 copy-start.9
  70.7 2.4 copy-start.12
  72.4 0.6 copy-start.3
  76.0 335.2 %all-reduce.7.cloned.1.call-start = ((), (), s32[]{:S(2)}) async-start(), calls=%async_computation.3 | async-start | bytes 2097152 | tf_op jit(solution)/shard_map/psum | solution.py:102
  236.1 15.6 %collective-permute-start.1 = (bf16[256,2048]{1,0:T(8,128)(2,1)}, bf16[256,2048]{1,0:T(8,128)(2,1)S(1)}, u32[]{:S(2)}, u32[]{:S(2)}) collective-permute-start(bf16[256,2048]{1,0:T(8,128)(2,1)} %all-reduce.5.cloned.1.call-done), channel_id=1, source_target_pairs={{0,16},{16,0},{32,48},{48,32},{64,80},{80,64},{96,112},{112,96},{1... | collective-permute-start | bytes 3145736 | tf_op jit(solution)/shard_map/ppermute | solution.py:17
  253.5 1.3 copy-start.1
  253.5 2.0 copy-start.10
  255.5 176.3 %copy-start.8 = (bf16[2,8,2048]{2,1,0:T(8,128)(2,1)S(1)}, bf16[2,8,2048]{2,1,0:T(8,128)(2,1)}, u32[]{:S(2)}) copy-start(bf16[2,8,2048]{2,1,0:T(8,128)(2,1)} %param.12) | copy-start | bytes 196612
  257.0 181.7 %copy-start.4 = (bf16[256,1,192]{0,2,1:T(8,128)(2,1)S(1)}, bf16[256,1,192]{0,2,1:T(8,128)(2,1)}, u32[]{:S(2)}) copy-start(bf16[256,1,192]{0,2,1:T(8,128)(2,1)} %copy-done.3) | copy-start | bytes 294916
  257.0 181.8 %copy-start.13 = (f32[1,64,64]{2,1,0:T(8,128)S(1)}, f32[1,64,64]{2,1,0:T(8,128)}, u32[]{:S(2)}) copy-start(f32[1,64,64]{2,1,0:T(8,128)} %param.19) | copy-start | bytes 49156
  411.2 15.6 %collective-permute-start.2 = (bf16[256,2048]{1,0:T(8,128)(2,1)}, bf16[256,2048]{1,0:T(8,128)(2,1)S(1)}, u32[]{:S(2)}, u32[]{:S(2)}) collective-permute-start(bf16[256,2048]{1,0:T(8,128)(2,1)} %all-reduce.7.cloned.1.call-done), channel_id=1, source_target_pairs={{0,16},{16,0},{32,48},{48,32},{64,80},{80,64},{96,112},{112,96},{1... | collective-permute-start | bytes 3145736 | tf_op jit(solution)/shard_map/ppermute | solution.py:17
  427.7 58.2 %copy-start.7 = (bf16[8,2048]{1,0:T(8,128)(2,1)}, bf16[8,2048]{1,0:T(8,128)(2,1)S(1)}, u32[]{:S(2)}) copy-start(bf16[8,2048]{1,0:T(8,128)(2,1)S(1)} %fusion.77) | copy-start | bytes 98308
  427.7 4.1 collective-permute-start.3
  432.7 51.9 %all-to-all-start.1 = ((bf16[16,8,2048]{2,1,0:T(8,128)(2,1)}), bf16[16,8,2048]{2,1,0:T(8,128)(2,1)}, u32[]{:S(2)}, u32[]{:S(2)}) async-start(bf16[16,8,2048]{2,1,0:T(8,128)(2,1)} %stack.5), calls=%async_computation.1 | async-start | bytes 1048576 | tf_op jit(solution)/shard_map/all_to_all | solution.py:10
  438.6 215.4 %all-reduce.9.cloned.1.call-start = ((), (), s32[]{:S(2)}) async-start(), calls=%async_computation.4 | async-start | bytes 2097152 | tf_op jit(solution)/shard_map/psum | solution.py:102
  439.5 4.2 collective-permute-start.4
  486.2 2.4 copy-start.14
  487.9 0.6 copy-start.5
  491.6 337.7 %all-reduce.11.cloned.1.call-start = ((), (), s32[]{:S(2)}) async-start(), calls=%async_computation.5 | async-start | bytes 2097152 | tf_op jit(solution)/shard_map/psum | solution.py:102
  654.0 15.6 %collective-permute-start.5 = (bf16[256,2048]{1,0:T(8,128)(2,1)}, bf16[256,2048]{1,0:T(8,128)(2,1)S(1)}, u32[]{:S(2)}, u32[]{:S(2)}) collective-permute-start(bf16[256,2048]{1,0:T(8,128)(2,1)} %all-reduce.9.cloned.1.call-done), channel_id=1, source_target_pairs={{0,16},{16,0},{32,48},{48,32},{64,80},{80,64},{96,112},{112,96},{1... | collective-permute-start | bytes 3145736 | tf_op jit(solution)/shard_map/ppermute | solution.py:17
  671.4 1.3 copy-start.2
  671.4 2.0 copy-start.11
  673.4 168.9 %copy-start.6 = (bf16[256,1,192]{0,2,1:T(8,128)(2,1)S(1)}, bf16[256,1,192]{0,2,1:T(8,128)(2,1)}, u32[]{:S(2)}) copy-start(bf16[256,1,192]{0,2,1:T(8,128)(2,1)} %copy-done.5) | copy-start | bytes 294916
  673.4 169.6 %copy-start.15 = (f32[1,64,64]{2,1,0:T(8,128)S(1)}, f32[1,64,64]{2,1,0:T(8,128)}, u32[]{:S(2)}) copy-start(f32[1,64,64]{2,1,0:T(8,128)} %fusion.26) | copy-start | bytes 49156
  829.2 15.6 %collective-permute-start.6 = (bf16[256,2048]{1,0:T(8,128)(2,1)}, bf16[256,2048]{1,0:T(8,128)(2,1)S(1)}, u32[]{:S(2)}, u32[]{:S(2)}) collective-permute-start(bf16[256,2048]{1,0:T(8,128)(2,1)} %all-reduce.11.cloned.1.call-done), channel_id=1, source_target_pairs={{0,16},{16,0},{32,48},{48,32},{64,80},{80,64},{96,112},{112,96},{1... | collective-permute-start | bytes 3145736 | tf_op jit(solution)/shard_map/ppermute | solution.py:17
Sparse Core Ops, SparseCore 0:
  76.1 159.9 all-reduce.4
  257.1 154.0 all-reduce.6
  491.7 162.3 all-reduce.8
  675.0 154.1 all-reduce.10
